TPU v7x, 256 devices: a whole 4x4x8 slice. The times are simulated.
256 devices in a mesh: trow: 16 (over x, y), tcol: 8 (over z), rep: 2 (over core).
Axes of the slice: x: 4, y: 4, z: 8, core: 2. Of those that a mesh axis runs over, the one named last changes fastest.
Arguments:
- users: float32 [131072, 128], P(('trow', 'tcol'))
- items: float32 [65536, 128], P(('tcol', 'trow'))
- ratings: bfloat16 [16, 8, 2, 64, 128, 128], P('trow', 'tcol', 'rep'), may hold values from -6 to 6
- row_mask: int32 [16, 8, 2, 64, 128], P('trow', 'tcol', 'rep'), may hold values 0 or 1
- col_mask: int32 [16, 8, 2, 64, 128], P('trow', 'tcol', 'rep'), may hold values 0 or 1
- row_slots: int32 [16, 8, 2, 64], P('trow', 'tcol', 'rep'), may hold values from 0 to 31, as said below
- col_slots: int32 [16, 8, 2, 64], P('trow', 'tcol', 'rep'), may hold values from 0 to 31, as said below
- send_users: int32 [16, 8, 2, 8, 4], P('trow', 'tcol', 'rep'), may hold values from 0 to 7, as said below
- send_items: int32 [16, 8, 2, 16, 2], P('trow', 'tcol', 'rep'), may hold values from 0 to 3, as said below
Outputs:
- users_out: float32 [131072, 128], P(('trow', 'tcol'))
- items_out: float32 [65536, 128], P(('tcol', 'trow'))
Inputs may be any that keep to these rules, and one draw needn't show every extreme that they name: `send_users`: distinct within each row of the last dimension. `send_items`: distinct within each row of the last dimension. `row_slots`: every slot is named by some tile of each device. `col_slots`: every slot is named by some tile of each device.
All inputs are finite; a program needn't handle non-finite values. No bound on the sum of `row_mask` or of `col_mask` on one device may be relied on, other than what follows from the above.
Results may differ from a plain program's by a relative error of at most 0.02.
Values may be sent and summed in bfloat16 or wider, within the bound.
A program may use at most 64 MiB of HBM per device.

v0:
```python
import jax
import jax.numpy as jnp
from jax import lax
from jax.sharding import PartitionSpec as P

ITERS = 2


def precondition(gradient, gramian):
    factor = jnp.linalg.cholesky(gramian)
    return jax.scipy.linalg.cho_solve((factor, True), gradient.T).T


def pool_sum(index_list, terms, pool_count):
    onehot = (
        lax.broadcasted_iota(jnp.int32, (pool_count, index_list.shape[0]), 0) == index_list[None, :]
    ).astype(jnp.bfloat16)
    flat = terms.reshape(terms.shape[0], -1)
    upper = flat.astype(jnp.bfloat16)
    lower = (flat - upper.astype(jnp.float32)).astype(jnp.bfloat16)
    return jnp.dot(onehot, upper, preferred_element_type=jnp.float32) + jnp.dot(
        onehot, lower, preferred_element_type=jnp.float32
    )


def on_device(
    users, items, ratings, row_mask, col_mask, row_slots, col_slots, send_users, send_items
):
    n_trow = lax.axis_size("trow")
    n_tcol = lax.axis_size("tcol")
    n_rep = lax.axis_size("rep")
    tile_size = ratings.shape[-1]
    rank_width = users.shape[1]
    tile_count = ratings.shape[3]
    own_users = users.shape[0] // tile_size
    own_items = items.shape[0] // tile_size
    user_cap = send_users.shape[-1]
    item_cap = send_items.shape[-1]
    ratings_local = ratings.reshape(tile_count, tile_size, tile_size)
    weights = (
        row_mask.reshape(tile_count, tile_size)[:, :, None]
        * col_mask.reshape(tile_count, tile_size)[:, None, :]
    ).astype(jnp.float32)
    row_slot_list = row_slots.reshape(-1)
    col_slot_list = col_slots.reshape(-1)
    user_sends = send_users.reshape(n_tcol, -1)
    item_sends = send_items.reshape(n_trow, -1)
    user_received = lax.all_to_all(
        user_sends, "tcol", split_axis=0, concat_axis=0, tiled=True
    ).reshape(-1)
    item_received = lax.all_to_all(
        item_sends, "trow", split_axis=0, concat_axis=0, tiled=True
    ).reshape(-1)
    row_list = row_slot_list // user_cap * own_users + user_received[row_slot_list]
    col_list = col_slot_list // item_cap * own_items + item_received[col_slot_list]
    all_users = own_users * tile_size * n_trow * n_tcol
    all_items = own_items * tile_size * n_trow * n_tcol
    user_coef = 2.0 * all_items * own_users / (tile_size * tile_count * n_rep)
    item_coef = 2.0 * all_users * own_items / (tile_size * tile_count * n_rep)
    for iteration in range(ITERS):
        gram_users, gram_items = lax.psum(
            (
                jnp.dot(
                    users.T,
                    users,
                    precision=lax.Precision.HIGHEST,
                    preferred_element_type=jnp.float32,
                ),
                jnp.dot(
                    items.T,
                    items,
                    precision=lax.Precision.HIGHEST,
                    preferred_element_type=jnp.float32,
                ),
            ),
            ("trow", "tcol"),
        )
        user_half = users.astype(jnp.bfloat16).reshape(own_users, tile_size, rank_width)
        item_half = items.astype(jnp.bfloat16).reshape(own_items, tile_size, rank_width)
        user_pool = lax.all_gather(user_half, "tcol", axis=0, tiled=True)
        item_pool = lax.all_gather(item_half, "trow", axis=0, tiled=True)
        x_tiles = user_pool[row_list]
        y_tiles = item_pool[col_list]
        predicted = jnp.einsum("tar,tbr->tab", x_tiles, y_tiles, preferred_element_type=jnp.float32)
        errors = (weights * (predicted - ratings_local.astype(jnp.float32))).astype(jnp.bfloat16)
        user_terms = jnp.einsum("tab,tbr->tar", errors, y_tiles, preferred_element_type=jnp.float32)
        item_terms = jnp.einsum("tab,tar->tbr", errors, x_tiles, preferred_element_type=jnp.float32)
        user_pooled = pool_sum(row_list, user_terms, user_pool.shape[0])
        item_pooled = pool_sum(col_list, item_terms, item_pool.shape[0])
        user_grad = lax.psum_scatter(user_pooled, "tcol", scatter_dimension=0, tiled=True)
        item_grad = lax.psum_scatter(item_pooled, "trow", scatter_dimension=0, tiled=True)
        user_grad, item_grad = lax.psum((user_grad, item_grad), "rep")
        new_users = users - user_coef * precondition(user_grad.reshape(-1, rank_width), gram_items)
        new_items = items - item_coef * precondition(item_grad.reshape(-1, rank_width), gram_users)
        users, items = (new_users, new_items)
    return (users, items)


def solution(mesh):
    return jax.shard_map(
        on_device,
        mesh=mesh,
        in_specs=(
            P(("trow", "tcol"), None),
            P(("tcol", "trow"), None),
            P("trow", "tcol", "rep", None, None, None),
            P("trow", "tcol", "rep", None, None),
            P("trow", "tcol", "rep", None, None),
            P("trow", "tcol", "rep", None),
            P("trow", "tcol", "rep", None),
            P("trow", "tcol", "rep", None, None),
            P("trow", "tcol", "rep", None, None),
        ),
        out_specs=(P(("trow", "tcol"), None), P(("tcol", "trow"), None)),
        check_vma=False,
    )
```

profile of v0, /device:TPU:1, one launch (start us, length us, event | category | flops | bytes accessed | tf_op | source)
XLA Modules:
  0.0 1075.5 jit_solution(2654260133140196737)
XLA Ops:
  7.2 1.8 convert_element_type.69
  9.1 1.6 convert_element_type.70
  10.7 1.3 copy.48
  12.1 7.6 all-to-all-start.1
  21.0 1.3 copy.47
  22.3 3.7 all-to-all-done.1
  26.1 8.2 all-to-all-start
  36.4 4.4 all-to-all-done
  42.3 9.4 all-gather.5.cloned.1.call-done
  51.7 3.7 gather_fusion.1
  55.4 50.8 %all-gather.7.cloned.1.call-done = bf16[64,128,128]{2,1,0:T(8,128)(2,1)} async-done(((bf16[4,128,128]{2,1,0:T(8,128)(2,1)}), bf16[64,128,128]{2,1,0:T(8,128)(2,1)}) %all-gather.7.cloned.1.call-update) | async-done | bytes 2097168 | tf_op jit(solution)/shard_map/all_gather | solution.py:81
  106.3 2.5 gather_fusion.3
  108.9 4.1 fusion.1
  114.4 2.8 fusion.9
  117.2 4.9 convolution_add_fusion.2
  122.3 2.3 fusion.59
  124.6 2.8 fusion.8
  127.4 4.9 convolution_add_fusion.3
  134.5 1.6 fusion.60
  137.4 98.5 %all-reduce.13.cloned.1.call-done = f32[64,16384]{1,0:T(8,128)} async-done(((f32[64,16384]{1,0:T(8,128)}), f32[64,16384]{1,0:T(8,128)}) %all-reduce.13.cloned.1.call-update) | async-done | bytes 4194320
  237.9 55.8 %reduce-scatter.3.cloned.1.call-done = f32[8,16384]{1,0:T(8,128)} async-done(((f32[64,16384]{1,0:T(8,128)}), f32[8,16384]{1,0:T(8,128)}) %reduce-scatter.3.cloned.1.call-update) | async-done | bytes 524304 | tf_op jit(solution)/shard_map/reduce_scatter | solution.py:90
  293.7 1.9 reshape.380
  296.1 209.1 %all-reduce.19.cloned.1.call-done = (f32[128,128]{0,1:T(8,128)}, f32[128,128]{0,1:T(8,128)}) async-done(((f32[128,128]{0,1:T(8,128)}, f32[128,128]{0,1:T(8,128)}), (f32[128,128]{0,1:T(8,128)}, f32[128,128]{0,1:T(8,128)})) %all-reduce.19.cloned.1.call-update) | async-done | bytes 131088 | tf_op jit(solution)/shard_map/psum | solution.py:61
  508.0 11.7 %cholesky.74 = f32[128,128]{1,0:T(8,128)S(1)} custom-call(f32[128,128]{1,0:T(8,128)S(1)} %get-tuple-element.24), custom_call_target="Cholesky" | custom-call | tf_op jit(solution)/shard_map/jit(cholesky)/cholesky | solution.py:10
  521.1 9.8 custom-call.14
  530.9 10.3 all-reduce.23.cloned.1.call-done
  541.2 1.7 fusion.41
  545.1 11.7 %cholesky.85 = f32[128,128]{1,0:T(8,128)S(1)} custom-call(f32[128,128]{1,0:T(8,128)S(1)} %get-tuple-element.23), custom_call_target="Cholesky" | custom-call | tf_op jit(solution)/shard_map/jit(cholesky)/cholesky | solution.py:10
  558.1 9.8 custom-call.15
  572.0 10.9 %all-gather.9.cloned.1.call-done = bf16[64,128,128]{2,1,0:T(8,128)(2,1)} async-done(((bf16[8,128,128]{2,1,0:T(8,128)(2,1)}), bf16[64,128,128]{2,1,0:T(8,128)(2,1)}) %all-gather.9.cloned.1.call-update) | async-done | bytes 2097168 | tf_op jit(solution)/shard_map/all_gather | solution.py:80
  582.9 3.7 gather_fusion.4
  586.7 50.5 %all-gather.11.cloned.1.call-done = bf16[64,128,128]{2,1,0:T(8,128)(2,1)} async-done(((bf16[4,128,128]{2,1,0:T(8,128)(2,1)}), bf16[64,128,128]{2,1,0:T(8,128)(2,1)}) %all-gather.11.cloned.1.call-update) | async-done | bytes 2097168 | tf_op jit(solution)/shard_map/all_gather | solution.py:81
  637.2 2.5 gather_fusion.5
  639.7 4.1 fusion.3
  645.2 2.8 fusion.11
  648.0 4.9 convolution_add_fusion
  653.0 2.3 fusion.63
  655.3 2.8 fusion.10
  658.1 4.9 convolution_add_fusion.1
  663.2 187.3 %all-reduce.17.cloned.1.call-done = (f32[128,128]{0,1:T(8,128)}, f32[128,128]{0,1:T(8,128)}) async-done(((f32[128,128]{0,1:T(8,128)}, f32[128,128]{0,1:T(8,128)}), (f32[128,128]{0,1:T(8,128)}, f32[128,128]{0,1:T(8,128)})) %all-reduce.17.cloned.1.call-update) | async-done | bytes 131088 | tf_op jit(solution)/shard_map/psum | solution.py:61
  852.4 11.7 %cholesky.96 = f32[128,128]{1,0:T(8,128)S(1)} custom-call(f32[128,128]{1,0:T(8,128)S(1)} %fusion.35), custom_call_target="Cholesky" | custom-call | tf_op jit(solution)/shard_map/jit(cholesky)/cholesky | solution.py:10
  864.8 104.5 %all-reduce.15.cloned.1.call-done = f32[64,16384]{1,0:T(8,128)} async-done(((f32[64,16384]{1,0:T(8,128)}), f32[64,16384]{1,0:T(8,128)}) %all-reduce.15.cloned.1.call-update) | async-done | bytes 4194320
  971.4 56.1 %reduce-scatter.5.cloned.1.call-done = f32[8,16384]{1,0:T(8,128)} async-done(((f32[64,16384]{1,0:T(8,128)}), f32[8,16384]{1,0:T(8,128)}) %reduce-scatter.5.cloned.1.call-update) | async-done | bytes 524304 | tf_op jit(solution)/shard_map/reduce_scatter | solution.py:90
  1027.5 1.9 reshape.387
  1030.1 9.8 custom-call.16
  1040.0 11.7 %cholesky.107 = f32[128,128]{1,0:T(8,128)S(1)} custom-call(f32[128,128]{1,0:T(8,128)S(1)} %fusion.31), custom_call_target="Cholesky" | custom-call | tf_op jit(solution)/shard_map/jit(cholesky)/cholesky | solution.py:10
  1053.2 10.0 custom-call.17
  1063.3 1.7 fusion.33
  (111 shorter events, 35.1 us)
Async XLA Ops:
  7.2 35.1 %copy-start.12 = (s32[1,1,1,64]{3,2,1,0:T(1,128)S(1)}, s32[1,1,1,64]{3,2,1,0:T(1,128)}, u32[]{:S(2)}) copy-start(s32[1,1,1,64]{3,2,1,0:T(1,128)} %param.19) | copy-start | bytes 772
  7.2 29.1 %copy-start.11 = (s32[1,1,1,64]{3,2,1,0:T(1,128)S(1)}, s32[1,1,1,64]{3,2,1,0:T(1,128)}, u32[]{:S(2)}) copy-start(s32[1,1,1,64]{3,2,1,0:T(1,128)} %param.20) | copy-start | bytes 772
  7.2 44.5 %all-gather.5.cloned.1.call-start = ((), (), s32[]{:S(2)}) async-start(), calls=%async_computation.4 | async-start | bytes 2359296 | tf_op jit(solution)/shard_map/all_gather | solution.py:80
  9.0 97.3 %all-gather.7.cloned.1.call-start = ((), (), s32[]{:S(2)}) async-start(), calls=%async_computation.5 | async-start | bytes 2228224 | tf_op jit(solution)/shard_map/all_gather | solution.py:81
  12.1 14.0 %all-to-all-start.1 = ((s32[16,1,2]{2,1,0:T(1,128)}), s32[16,1,2]{2,1,0:T(1,128)S(1)}, u32[]{:S(2)}, u32[]{:S(2)}) async-start(s32[16,1,2]{2,1,0:T(1,128)} %copy.48), calls=%async_computation.1 | async-start | bytes 16384 | tf_op jit(solution)/shard_map/all_to_all | solution.py:51
  26.1 14.7 %all-to-all-start = ((s32[8,1,4]{2,1,0:T(1,128)}), s32[8,1,4]{2,1,0:T(1,128)S(1)}, u32[]{:S(2)}, u32[]{:S(2)}) async-start(s32[8,1,4]{2,1,0:T(1,128)} %copy.47), calls=%async_computation | async-start | bytes 8192 | tf_op jit(solution)/shard_map/all_to_all | solution.py:48
  34.3 201.6 %all-reduce.13.cloned.1.call-start = ((), (), s32[]{:S(2)}) async-start(), calls=%async_computation.10 | async-start | bytes 8388608
  55.4 53.4 %copy-start.9 = (s32[1,1,1,64,128]{4,3,2,1,0:T(8,128)S(1)}, s32[1,1,1,64,128]{4,3,2,1,0:T(8,128)}, u32[]{:S(2)}) copy-start(s32[1,1,1,64,128]{4,3,2,1,0:T(8,128)} %param.18) | copy-start | bytes 98308
  55.4 53.4 %copy-start.10 = (s32[1,1,1,64,128]{4,3,2,1,0:T(8,128)S(1)}, s32[1,1,1,64,128]{4,3,2,1,0:T(8,128)}, u32[]{:S(2)}) copy-start(s32[1,1,1,64,128]{4,3,2,1,0:T(8,128)} %param.17) | copy-start | bytes 98308
  108.9 4.1 copy-start.1
  113.0 1.4 copy-start.2
  122.1 171.6 %reduce-scatter.3.cloned.1.call-start = ((), (), s32[]{:S(2)}) async-start(), calls=%async_computation.6 | async-start | bytes 4718592 | tf_op jit(solution)/shard_map/reduce_scatter | solution.py:90
  132.3 1.0 copy-start.5
  132.3 2.2 copy-start.4
  132.3 3.9 copy-start.13
  132.3 372.9 %all-reduce.19.cloned.1.call-start = ((), (), s32[]{:S(2)}) async-start(), calls=%async_computation.13 | async-start | bytes 262144 | tf_op jit(solution)/shard_map/psum | solution.py:61
  136.1 405.1 %all-reduce.23.cloned.1.call-start = ((), (), s32[]{:S(2)}) async-start(), calls=%async_computation.15 | async-start | bytes 1572864 | tf_op jit(solution)/shard_map/psum | solution.py:92
  295.6 287.3 %all-gather.9.cloned.1.call-start = ((), (), s32[]{:S(2)}) async-start(), calls=%async_computation.7 | async-start | bytes 2359296 | tf_op jit(solution)/shard_map/all_gather | solution.py:80
  541.2 26.7 %copy-start.7 = (f32[128,512]{0,1:T(8,128)S(1)}, f32[128,512]{0,1:T(8,128)}, u32[]{:S(2)}) copy-start(f32[128,512]{0,1:T(8,128)} %get-tuple-element.18) | copy-start | bytes 786436
  544.4 92.8 %all-gather.11.cloned.1.call-start = ((), (), s32[]{:S(2)}) async-start(), calls=%async_computation.8 | async-start | bytes 2228224 | tf_op jit(solution)/shard_map/all_gather | solution.py:81
  569.5 281.0 %all-reduce.17.cloned.1.call-start = ((), (), s32[]{:S(2)}) async-start(), calls=%async_computation.12 | async-start | bytes 262144 | tf_op jit(solution)/shard_map/psum | solution.py:61
  571.8 397.6 %all-reduce.15.cloned.1.call-start = ((), (), s32[]{:S(2)}) async-start(), calls=%async_computation.11 | async-start | bytes 8388608
  639.7 4.1 copy-start
  643.9 1.4 copy-start.3
  652.9 374.5 %reduce-scatter.5.cloned.1.call-start = ((), (), s32[]{:S(2)}) async-start(), calls=%async_computation.9 | async-start | bytes 4718592 | tf_op jit(solution)/shard_map/reduce_scatter | solution.py:90
  663.0 400.3 %all-reduce.21.cloned.1.call-start = ((), (), s32[]{:S(2)}) async-start(), calls=%async_computation.14 | async-start | bytes 1572864 | tf_op jit(solution)/shard_map/psum | solution.py:92
  850.6 189.4 %copy-start.6 = (f32[128,128]{0,1:T(8,128)S(1)}, f32[128,128]{0,1:T(8,128)}, u32[]{:S(2)}) copy-start(f32[128,128]{0,1:T(8,128)} %get-tuple-element.12) | copy-start | bytes 196612
  1063.2 3.3 copy-start.8
Sparse Core Ops, SparseCore 0:
  10.4 41.2 all-gather.4
  54.7 51.5 all-gather.6
  122.2 113.6 all-reduce.12
  238.3 55.3 reduce-scatter.2
  299.1 206.1 all-reduce.18
  508.5 32.6 all-reduce.22
  544.5 38.3 all-gather.8
  585.9 51.1 all-gather.10
  642.7 207.7 all-reduce.16
  854.1 115.2 all-reduce.14
  972.1 55.3 reduce-scatter.4
  1030.7 29.7 all-reduce.20
where the time goes:
time: 1080 us
  waiting for transfers between devices  852 us (79%)
  other arithmetic  99.6 us (9%)
  matrix products  56.4 us (5%)
  local copies, waits for them, and re-layouts  34.4 us (3%)
  starting transfers between devices  17.6 us (2%)
  between operations  15.7 us (1%)
    psum x2, waiting for transfers between devices, on_device(): lax.psum((jnp.dot(users.T, users, precision=lax.Precision.HIGHEST, prefer...  396 us
    unnamed x14, waiting for transfers between devices  203 us
    reduce_scatter x2, waiting for transfers between devices, on_device(): lax.psum_scatter(user_pooled, 'tcol', scatter_dimension=0, tiled=True)  112 us
    all_gather x2, waiting for transfers between devices, on_device(): item_pool = lax.all_gather(item_half, 'trow', axis=0, tiled=True)  101 us
    another operation x12, other arithmetic, precondition(): factor = jnp.linalg.cholesky(gramian)  49.7 us
    another operation x8, other arithmetic, precondition(): return jax.scipy.linalg.cho_solve((factor, True), gradient.T).T  42.1 us
  transfers between devices with their start and end apart: 14, of which 13 were waited for; matrix products, arithmetic and copies ran while one was open for 15% of the time, Pallas kernels for 0%

commit v1 on v0

--- a/solution.py
+++ b/solution.py
@@ -78,7 +78,10 @@
         user_half = users.astype(jnp.bfloat16).reshape(own_users, tile_size, rank_width)
         item_half = items.astype(jnp.bfloat16).reshape(own_items, tile_size, rank_width)
         user_pool = lax.all_gather(user_half, "tcol", axis=0, tiled=True)
-        item_pool = lax.all_gather(item_half, "trow", axis=0, tiled=True)
+        placed = lax.axis_size("trow")
+        g_now = jnp.stack(placed * [item_half])
+        q_next = lax.all_to_all(g_now, axis_name="trow", split_axis=0, concat_axis=0)
+        item_pool = jnp.concatenate(q_next, 0)
         x_tiles = user_pool[row_list]
         y_tiles = item_pool[col_list]
         predicted = jnp.einsum("tar,tbr->tab", x_tiles, y_tiles, preferred_element_type=jnp.float32)

time: 1080 us -> 1000 us (0.926)
  waiting for transfers between devices: 852 us -> 754 us
    all_gather x2 -> x0, waiting for transfers between devices: 101 us -> none  [on_device(): item_pool = lax.all_gather(item_half, 'trow', axis=0, tiled=True)]
    all_to_all x0 -> x2, waiting for transfers between devices: none -> 48.2 us  [on_device(): lax.all_to_all(g_now, axis_name='trow', split_axis=0, concat_axis=0)]
    psum x2, waiting for transfers between devices: 396 us -> 371 us  [on_device(): lax.psum((jnp.dot(users.T, users, precision=lax.Precision.HIGHEST, prefer...]
    all_gather x2, waiting for transfers between devices: 20.3 us -> 0.04 us  [on_device(): user_pool = lax.all_gather(user_half, 'tcol', axis=0, tiled=True)]
    unnamed x14 -> x12, waiting for transfers between devices: 203 us -> 202 us
  transfers between devices with their start and end apart: 14 -> 14, of which waited for: 13 -> 11; matrix products, arithmetic and copies ran while one was open for 15% -> 16% of each run, Pallas kernels for 0% -> 0%
where the time goes in v1:
time: 1000 us; the launch traced here: 992 us
  waiting for transfers between devices  754 us (75%)
  other arithmetic  97.9 us (10%)
  matrix products  56.4 us (6%)
  local copies, waits for them, and re-layouts  40.1 us (4%)
  starting transfers between devices  27.2 us (3%)
  between operations  15.8 us (2%)
    psum x2, waiting for transfers between devices, on_device(): lax.psum((jnp.dot(users.T, users, precision=lax.Precision.HIGHEST, prefer...  371 us
    unnamed x12, waiting for transfers between devices  202 us
    reduce_scatter x2, waiting for transfers between devices, on_device(): lax.psum_scatter(user_pooled, 'tcol', scatter_dimension=0, tiled=True)  112 us
    another operation x12, other arithmetic, precondition(): factor = jnp.linalg.cholesky(gramian)  49.7 us
    all_to_all x2, waiting for transfers between devices, on_device(): lax.all_to_all(g_now, axis_name='trow', split_axis=0, concat_axis=0)  48.2 us
    another operation x8, other arithmetic, precondition(): return jax.scipy.linalg.cho_solve((factor, True), gradient.T).T  42.3 us
  transfers between devices with their start and end apart: 14, of which 11 were waited for; matrix products, arithmetic and copies ran while one was open for 16% of the time, Pallas kernels for 0%

profile of v1, /device:TPU:1, one launch (start us, length us, event | category | flops | bytes accessed | tf_op | source)
XLA Modules:
  0.0 991.8 jit_solution(119803367789662200)
XLA Ops:
  7.2 1.8 convert_element_type.69
  9.0 1.4 copy.49
  10.4 7.6 all-to-all-start.2
  19.3 5.0 all-to-all-done.2
  24.3 8.2 all-to-all-start
  33.4 5.7 all-to-all-done
  39.1 1.8 stack.6
  40.9 3.9 all-to-all-start.1
  48.6 21.3 %all-to-all-done.1 = bf16[16,4,128,128]{3,2,1,0:T(8,128)(2,1)S(1)} async-done(((bf16[16,4,128,128]{3,2,1,0:T(8,128)(2,1)}), bf16[16,4,128,128]{3,2,1,0:T(8,128)(2,1)S(1)}, u32[]{:S(2)}, u32[]{:S(2)}) %all-to-all-start.1) | async-done | bytes 2097184 | tf_op jit(solution)/shard_map/all_to_all | solution.py:83
  71.2 2.5 gather_fusion.3
  73.8 3.7 gather_fusion.1
  77.5 4.1 fusion.1
  83.0 2.8 fusion.9
  85.8 4.9 convolution_add_fusion.2
  91.0 2.3 fusion.59
  93.3 2.8 fusion.8
  96.1 4.9 convolution_add_fusion.3
  103.2 1.6 fusion.60
  106.1 97.3 %all-reduce.13.cloned.1.call-done = f32[64,16384]{1,0:T(8,128)} async-done(((f32[64,16384]{1,0:T(8,128)}), f32[64,16384]{1,0:T(8,128)}) %all-reduce.13.cloned.1.call-update) | async-done | bytes 4194320
  205.4 55.9 %reduce-scatter.3.cloned.1.call-done = f32[8,16384]{1,0:T(8,128)} async-done(((f32[64,16384]{1,0:T(8,128)}), f32[8,16384]{1,0:T(8,128)}) %reduce-scatter.3.cloned.1.call-update) | async-done | bytes 524304 | tf_op jit(solution)/shard_map/reduce_scatter | solution.py:93
  261.4 1.9 reshape.384
  264.0 208.9 %all-reduce.19.cloned.1.call-done = (f32[128,128]{0,1:T(8,128)}, f32[128,128]{0,1:T(8,128)}) async-done(((f32[128,128]{0,1:T(8,128)}, f32[128,128]{0,1:T(8,128)}), (f32[128,128]{0,1:T(8,128)}, f32[128,128]{0,1:T(8,128)})) %all-reduce.19.cloned.1.call-update) | async-done | bytes 131088 | tf_op jit(solution)/shard_map/psum | solution.py:61
  475.7 11.7 %cholesky.74 = f32[128,128]{1,0:T(8,128)S(1)} custom-call(f32[128,128]{1,0:T(8,128)S(1)} %get-tuple-element.24), custom_call_target="Cholesky" | custom-call | tf_op jit(solution)/shard_map/jit(cholesky)/cholesky | solution.py:10
  488.8 9.8 custom-call.14
  498.6 10.3 %all-reduce.23.cloned.1.call-done = (f32[128,1024]{0,1:T(8,128)}, f32[128,512]{0,1:T(8,128)}) async-done(((f32[128,1024]{0,1:T(8,128)}, f32[128,512]{0,1:T(8,128)}), (f32[128,1024]{0,1:T(8,128)}, f32[128,512]{0,1:T(8,128)})) %all-reduce.23.cloned.1.call-update) | async-done | bytes 786448 | tf_op jit(solution)/shard_map/psum | solution.py:95
  508.9 1.7 fusion.41
  512.2 11.7 %cholesky.85 = f32[128,128]{1,0:T(8,128)S(1)} custom-call(f32[128,128]{1,0:T(8,128)S(1)} %get-tuple-element.23), custom_call_target="Cholesky" | custom-call | tf_op jit(solution)/shard_map/jit(cholesky)/cholesky | solution.py:10
  525.3 9.9 %custom-call.15 = f32[1,128,128]{1,2,0:T(8,128)S(1)} custom-call(f32[1,128,128]{2,1,0:T(8,128)S(1)} %fusion.25), custom_call_target="InvertDiagBlocksLowerTriangular" | custom-call | tf_op jit(solution)/shard_map/jit(_cho_solve)/triangular_solve | solution.py:11
  536.2 1.8 stack.7
  538.0 6.3 all-to-all-start.3
  546.6 26.9 %all-to-all-done.3 = bf16[16,4,128,128]{3,2,1,0:T(8,128)(2,1)S(1)} async-done(((bf16[16,4,128,128]{3,2,1,0:T(8,128)(2,1)}), bf16[16,4,128,128]{3,2,1,0:T(8,128)(2,1)S(1)}, u32[]{:S(2)}, u32[]{:S(2)}) %all-to-all-start.3) | async-done | bytes 2097184 | tf_op jit(solution)/shard_map/all_to_all | solution.py:83
  574.8 2.5 gather_fusion.5
  577.4 3.7 gather_fusion.4
  581.2 4.1 fusion.3
  586.7 2.8 fusion.11
  589.5 4.9 convolution_add_fusion
  594.4 2.3 fusion.63
  596.7 2.8 fusion.10
  599.5 4.9 convolution_add_fusion.1
  604.6 162.0 %all-reduce.17.cloned.1.call-done = (f32[128,128]{0,1:T(8,128)}, f32[128,128]{0,1:T(8,128)}) async-done(((f32[128,128]{0,1:T(8,128)}, f32[128,128]{0,1:T(8,128)}), (f32[128,128]{0,1:T(8,128)}, f32[128,128]{0,1:T(8,128)})) %all-reduce.17.cloned.1.call-update) | async-done | bytes 131088 | tf_op jit(solution)/shard_map/psum | solution.py:61
  768.5 11.7 %cholesky.96 = f32[128,128]{1,0:T(8,128)S(1)} custom-call(f32[128,128]{1,0:T(8,128)S(1)} %fusion.35), custom_call_target="Cholesky" | custom-call | tf_op jit(solution)/shard_map/jit(cholesky)/cholesky | solution.py:10
  781.0 104.7 %all-reduce.15.cloned.1.call-done = f32[64,16384]{1,0:T(8,128)} async-done(((f32[64,16384]{1,0:T(8,128)}), f32[64,16384]{1,0:T(8,128)}) %all-reduce.15.cloned.1.call-update) | async-done | bytes 4194320
  887.7 56.1 %reduce-scatter.5.cloned.1.call-done = f32[8,16384]{1,0:T(8,128)} async-done(((f32[64,16384]{1,0:T(8,128)}), f32[8,16384]{1,0:T(8,128)}) %reduce-scatter.5.cloned.1.call-update) | async-done | bytes 524304 | tf_op jit(solution)/shard_map/reduce_scatter | solution.py:93
  943.8 1.9 reshape.391
  946.4 9.8 custom-call.16
  956.3 11.7 %cholesky.107 = f32[128,128]{1,0:T(8,128)S(1)} custom-call(f32[128,128]{1,0:T(8,128)S(1)} %fusion.31), custom_call_target="Cholesky" | custom-call | tf_op jit(solution)/shard_map/jit(cholesky)/cholesky | solution.py:10
  969.5 10.0 %custom-call.17 = f32[1,128,128]{1,2,0:T(8,128)S(1)} custom-call(f32[1,128,128]{2,1,0:T(8,128)S(1)} %fusion.27), custom_call_target="InvertDiagBlocksLowerTriangular" | custom-call | tf_op jit(solution)/shard_map/jit(_cho_solve)/triangular_solve | solution.py:11
  979.5 1.7 fusion.33
  (115 shorter events, 37.9 us)
Async XLA Ops:
  7.2 66.6 %all-gather.3.cloned.1.call-start = ((), (), s32[]{:S(2)}) async-start(), calls=%async_computation.6 | async-start | bytes 2359296 | tf_op jit(solution)/shard_map/all_gather | solution.py:80
  10.4 13.9 %all-to-all-start.2 = ((s32[16,1,2]{2,1,0:T(1,128)}), s32[16,1,2]{2,1,0:T(1,128)S(1)}, u32[]{:S(2)}, u32[]{:S(2)}) async-start(s32[16,1,2]{2,1,0:T(1,128)} %copy.49), calls=%async_computation.2 | async-start | bytes 16384 | tf_op jit(solution)/shard_map/all_to_all | solution.py:51
  24.3 14.8 %all-to-all-start = ((s32[8,1,4]{2,1,0:T(1,128)}), s32[8,1,4]{2,1,0:T(1,128)S(1)}, u32[]{:S(2)}, u32[]{:S(2)}) async-start(s32[8,1,4]{2,1,0:T(1,128)} %copy.48), calls=%async_computation | async-start | bytes 8192 | tf_op jit(solution)/shard_map/all_to_all | solution.py:48
  40.9 3.9 copy-start.14
  40.9 4.0 copy-start.13
  40.9 28.9 %all-to-all-start.1 = ((bf16[16,4,128,128]{3,2,1,0:T(8,128)(2,1)}), bf16[16,4,128,128]{3,2,1,0:T(8,128)(2,1)S(1)}, u32[]{:S(2)}, u32[]{:S(2)}) async-start(bf16[16,4,128,128]{3,2,1,0:T(8,128)(2,1)} %stack.6), calls=%async_computation.1 | async-start | bytes 4194304 | tf_op jit(solution)/shard_map/all_to_all | solution.py:83
  44.8 158.7 %all-reduce.13.cloned.1.call-start = ((), (), s32[]{:S(2)}) async-start(), calls=%async_computation.10 | async-start | bytes 8388608
  69.9 1.3 copy-start.4
  73.7 3.8 copy-start.11
  73.7 3.8 copy-start.12
  77.5 4.1 copy-start.1
  81.6 1.4 copy-start.2
  90.7 170.7 %reduce-scatter.3.cloned.1.call-start = ((), (), s32[]{:S(2)}) async-start(), calls=%async_computation.7 | async-start | bytes 4718592 | tf_op jit(solution)/shard_map/reduce_scatter | solution.py:93
  100.9 1.0 copy-start.7
  100.9 2.2 copy-start.6
  100.9 3.9 copy-start.15
  101.0 372.0 %all-reduce.19.cloned.1.call-start = ((), (), s32[]{:S(2)}) async-start(), calls=%async_computation.13 | async-start | bytes 262144 | tf_op jit(solution)/shard_map/psum | solution.py:61
  104.8 404.1 %all-reduce.23.cloned.1.call-start = ((), (), s32[]{:S(2)}) async-start(), calls=%async_computation.15 | async-start | bytes 1572864 | tf_op jit(solution)/shard_map/psum | solution.py:95
  263.3 314.1 %all-gather.5.cloned.1.call-start = ((), (), s32[]{:S(2)}) async-start(), calls=%async_computation.8 | async-start | bytes 2359296 | tf_op jit(solution)/shard_map/all_gather | solution.py:80
  508.9 26.3 %copy-start.9 = (f32[128,512]{0,1:T(8,128)S(1)}, f32[128,512]{0,1:T(8,128)}, u32[]{:S(2)}) copy-start(f32[128,512]{0,1:T(8,128)} %get-tuple-element.18) | copy-start | bytes 786436
  538.0 35.5 %all-to-all-start.3 = ((bf16[16,4,128,128]{3,2,1,0:T(8,128)(2,1)}), bf16[16,4,128,128]{3,2,1,0:T(8,128)(2,1)S(1)}, u32[]{:S(2)}, u32[]{:S(2)}) async-start(bf16[16,4,128,128]{3,2,1,0:T(8,128)(2,1)} %stack.7), calls=%async_computation.4 | async-start | bytes 4194304 | tf_op jit(solution)/shard_map/all_to_all | solution.py:83
  544.3 222.4 %all-reduce.17.cloned.1.call-start = ((), (), s32[]{:S(2)}) async-start(), calls=%async_computation.12 | async-start | bytes 262144 | tf_op jit(solution)/shard_map/psum | solution.py:61
  546.6 339.1 %all-reduce.15.cloned.1.call-start = ((), (), s32[]{:S(2)}) async-start(), calls=%async_computation.11 | async-start | bytes 8388608
  573.5 1.3 copy-start.5
  581.2 4.1 copy-start
  585.3 1.4 copy-start.3
  594.3 349.4 %reduce-scatter.5.cloned.1.call-start = ((), (), s32[]{:S(2)}) async-start(), calls=%async_computation.9 | async-start | bytes 4718592 | tf_op jit(solution)/shard_map/reduce_scatter | solution.py:93
  604.4 375.2 %all-reduce.21.cloned.1.call-start = ((), (), s32[]{:S(2)}) async-start(), calls=%async_computation.14 | async-start | bytes 1572864 | tf_op jit(solution)/shard_map/psum | solution.py:95
  766.7 189.5 %copy-start.8 = (f32[128,128]{0,1:T(8,128)S(1)}, f32[128,128]{0,1:T(8,128)}, u32[]{:S(2)}) copy-start(f32[128,128]{0,1:T(8,128)} %get-tuple-element.12) | copy-start | bytes 196612
  979.5 3.3 copy-start.10
Sparse Core Ops, SparseCore 0:
  10.4 41.2 all-gather.2
  90.8 112.5 all-reduce.12
  206.0 55.3 reduce-scatter.2
  266.8 206.0 all-reduce.18
  476.2 32.6 all-reduce.22
  512.2 38.1 all-gather.4
  556.6 210.0 all-reduce.16
  770.4 115.2 all-reduce.14
  888.4 55.3 reduce-scatter.4
  947.0 29.7 all-reduce.20
